TPU v7x, 32 devices: a whole 2x2x4 slice. The times are simulated.
32 devices in a mesh: dp: 16 (over z, x, core), tensor: 2 (over y).
Axes of the slice: x: 2, y: 2, z: 4, core: 2. Of those that a mesh axis runs over, the one named last changes fastest.
Arguments:
- inputs: bfloat16 [3152, 768], P('dp'), may hold values from -6 to 6
- norm1_gain: float32 [768], replicated, may hold values from 0.5 to 1.5
- norm1_bias: float32 [768], replicated, may hold values from -4 to 4
- qkv_weight: bfloat16 [3, 768, 768], P(None, None, 'tensor'), may hold values from -0.21875 to 0.21875
- qv_bias: float32 [2, 768], P(None, 'tensor'), may hold values from -4 to 4
- proj_weight: bfloat16 [768, 768], P('tensor'), may hold values from -2 to 2
- proj_bias: float32 [768], replicated, may hold values from -4 to 4
- norm2_gain: float32 [768], replicated, may hold values from 0.5 to 1.5
- norm2_bias: float32 [768], replicated, may hold values from -4 to 4
- router: bfloat16 [768, 16], replicated, may hold values from -0.21582031 to 0.21582031
- expert_in: bfloat16 [16, 768, 3072], P('dp', None, 'tensor'), may hold values from -0.21875 to 0.21875
- expert_in_bias: float32 [16, 3072], P('dp', 'tensor'), may hold values from -4 to 4
- expert_out: bfloat16 [16, 3072, 768], P('dp', 'tensor'), may hold values from -0.109375 to 0.109375
- expert_out_bias: float32 [16, 768], replicated, may hold values from -4 to 4
- routes: int32 [3152, 2], P('dp'), may hold values from 0 to 15, all different within a row; in each aligned block of 197 rows (0 to 196, 197 to 393, ...) at most 42 rows name the same one
- cotangent: bfloat16 [3152, 768], P('dp'), may hold values from -6 to 6
Outputs:
- output: bfloat16 [3152, 768], P('dp')
- input_grad: float32 [3152, 768], P('dp')
- norm1_gain_grad: float32 [768], replicated
- norm1_bias_grad: float32 [768], replicated
- qkv_grad: float32 [3, 768, 768], P(None, None, 'tensor')
- qv_bias_grad: float32 [2, 768], P(None, 'tensor')
- proj_grad: float32 [768, 768], P('tensor')
- proj_bias_grad: float32 [768], replicated
- norm2_gain_grad: float32 [768], replicated
- norm2_bias_grad: float32 [768], replicated
- router_grad: float32 [768, 16], replicated
- expert_in_grad: float32 [16, 768, 3072], P('dp', None, 'tensor')
- expert_in_bias_grad: float32 [16, 3072], P('dp', 'tensor')
- expert_out_grad: float32 [16, 3072, 768], P('dp', 'tensor')
- expert_out_bias_grad: float32 [16, 768], replicated
Inputs may be any that keep to these rules, and one draw needn't show every extreme that they name: `routes`: each token names two different experts; among the tokens of one aligned block of 197 no expert is named more than 42 times, and in some block one expert is named exactly 42 times.
All inputs are finite; a program needn't handle non-finite values.
Results may differ from a plain program's by a relative error of at most 0.011.
Values may be sent and summed in bfloat16 or wider, within the bound.
No kernel may reach another device: no remote copies, remote signals or barrier semaphores. Data moves between devices by JAX's collectives and lax.ppermute only.
A program may use at most 192 MiB of HBM per device.

v0:
```python
import jax
import jax.numpy as jnp
from jax import lax
from jax.sharding import PartitionSpec as P

HEAD = 64
SEQ = 197
epsilon = 1e-06


def norm_parts(values):
    average = jnp.mean(values, axis=-1, keepdims=True)
    centred = values - average
    inverse = lax.rsqrt(jnp.mean(centred * centred, axis=-1, keepdims=True) + epsilon)
    return (centred * inverse, inverse)


def norm_back(inner_grad, normed, inverse):
    first_mean = jnp.mean(inner_grad, axis=-1, keepdims=True)
    second_mean = jnp.mean(inner_grad * normed, axis=-1, keepdims=True)
    return inverse * (inner_grad - first_mean - normed * second_mean)


def gelu_parts(pre_act):
    normal_cdf = 0.5 * (1.0 + lax.erf(pre_act * 0.7071067811865476))
    density = jnp.exp(-0.5 * pre_act * pre_act) * 0.3989422804014327
    return (pre_act * normal_cdf, normal_cdf + pre_act * density)


def local(
    inputs,
    norm1_gain,
    norm1_bias,
    qkv_weight,
    qv_bias,
    proj_weight,
    proj_bias,
    norm2_gain,
    norm2_bias,
    router,
    expert_in,
    expert_in_bias,
    expert_out,
    expert_out_bias,
    routes,
    cotangent,
):
    tok_count = inputs.shape[0]
    feat_dim = inputs.shape[1]
    head_cols = qkv_weight.shape[2]
    heads_here = head_cols // HEAD
    images = tok_count // SEQ
    experts = router.shape[1]
    sources = lax.axis_size("dp")
    group_size = sources // experts
    capacity = max(2, (10 * tok_count + 3 * experts - 1) // (3 * experts))
    score_scale = HEAD ** (-0.5)
    x_in = inputs.astype(jnp.float32)
    normed1, inverse1 = norm_parts(x_in)
    hidden1 = (normed1 * norm1_gain + norm1_bias).astype(jnp.bfloat16)
    projected = jnp.einsum("td,jde->jte", hidden1, qkv_weight, preferred_element_type=jnp.float32)
    bias_rows = jnp.stack([qv_bias[0], jnp.zeros_like(qv_bias[0]), qv_bias[1]])
    projected = (projected + bias_rows[:, None, :]).astype(jnp.bfloat16)
    heads_view = projected.reshape(3, images, SEQ, heads_here, HEAD)
    queries, key_vals, values_in = (heads_view[0], heads_view[1], heads_view[2])
    scores = (
        jnp.einsum("bqhd,bkhd->bhqk", queries, key_vals, preferred_element_type=jnp.float32)
        * score_scale
    )
    row_max = jnp.max(scores, axis=-1, keepdims=True)
    exp_scores = jnp.exp(scores - row_max)
    row_total = jnp.sum(exp_scores, axis=-1, keepdims=True)
    log_total = row_max + jnp.log(row_total)
    prob_low = (exp_scores / row_total).astype(jnp.bfloat16)
    attended = jnp.einsum(
        "bhqk,bkhd->bqhd", prob_low, values_in, preferred_element_type=jnp.float32
    )
    attended = attended.reshape(tok_count, head_cols).astype(jnp.bfloat16)
    attn_part = jnp.dot(attended, proj_weight, preferred_element_type=jnp.float32)
    middle = x_in + lax.psum(attn_part, "tensor") + proj_bias
    normed2, inverse2 = norm_parts(middle)
    hidden2 = (normed2 * norm2_gain + norm2_bias).astype(jnp.bfloat16)
    logits = jnp.dot(hidden2, router, preferred_element_type=jnp.float32)
    expert_ids = jnp.arange(experts, dtype=jnp.int32)
    pick_mask = (routes[:, :, None] == expert_ids[None, None, :]).astype(jnp.float32)
    chosen = jnp.sum(pick_mask * logits[:, None, :], axis=-1)
    chosen_max = jnp.max(chosen, axis=1, keepdims=True)
    chosen_exp = jnp.exp(chosen - chosen_max)
    gate_vals = chosen_exp / jnp.sum(chosen_exp, axis=1, keepdims=True)
    flat_routes = routes.reshape(-1)
    onehot = (flat_routes[:, None] == expert_ids[None, :]).astype(jnp.int32)
    rank_vals = jnp.sum(onehot * (jnp.cumsum(onehot, axis=0) - 1), axis=1)
    slot_index = flat_routes * capacity + rank_vals
    send_rows = jnp.zeros((experts * capacity, feat_dim), jnp.bfloat16)
    send_rows = send_rows.at[slot_index].set(jnp.repeat(hidden2, 2, axis=0))
    send_all = jnp.repeat(send_rows.reshape(experts, capacity, feat_dim), group_size, axis=0)
    arrived = lax.all_to_all(send_all, "dp", split_axis=0, concat_axis=0, tiled=True)
    arrived_flat = arrived.reshape(-1, feat_dim)
    pre_act = (
        jnp.dot(arrived_flat, expert_in[0], preferred_element_type=jnp.float32) + expert_in_bias[0]
    )
    activ_vals, gelu_slope = gelu_parts(pre_act)
    activ_low = activ_vals.astype(jnp.bfloat16)
    part_out = jnp.dot(activ_low, expert_out[0], preferred_element_type=jnp.float32).reshape(
        sources, capacity, feat_dim
    )
    came_back = lax.all_to_all(part_out, "dp", split_axis=0, concat_axis=0, tiled=True)
    local_rows = jnp.sum(came_back.reshape(experts, group_size, capacity, feat_dim), axis=1)
    full_rows = lax.psum(local_rows, "tensor") + expert_out_bias[:, None, :]
    result_rows = full_rows.astype(jnp.bfloat16)
    picked = (
        result_rows.reshape(-1, feat_dim)[slot_index]
        .reshape(tok_count, 2, feat_dim)
        .astype(jnp.float32)
    )
    output = (middle + jnp.sum(gate_vals[:, :, None] * picked, axis=1)).astype(jnp.bfloat16)
    grad_out = cotangent.astype(jnp.float32)
    gate_grad = jnp.sum(picked * grad_out[:, None, :], axis=-1)
    chosen_grad = gate_vals * (gate_grad - jnp.sum(gate_vals * gate_grad, axis=1, keepdims=True))
    logit_grad = jnp.sum(pick_mask * chosen_grad[:, :, None], axis=1).astype(jnp.bfloat16)
    row_grad = (
        (gate_vals[:, :, None] * grad_out[:, None, :]).astype(jnp.bfloat16).reshape(-1, feat_dim)
    )
    out_bias_grad = jnp.einsum(
        "re,rd->ed", onehot.astype(jnp.bfloat16), row_grad, preferred_element_type=jnp.float32
    )
    send_grad = jnp.zeros((experts * capacity, feat_dim), jnp.bfloat16).at[slot_index].set(row_grad)
    send_grad_all = jnp.repeat(send_grad.reshape(experts, capacity, feat_dim), group_size, axis=0)
    grad_arrived = lax.all_to_all(send_grad_all, "dp", split_axis=0, concat_axis=0, tiled=True)
    grad_arrived = grad_arrived.reshape(-1, feat_dim)
    out_weight_grad = jnp.einsum(
        "rf,rd->fd", activ_low, grad_arrived, preferred_element_type=jnp.float32
    )
    act_grad = (
        jnp.einsum("rd,fd->rf", grad_arrived, expert_out[0], preferred_element_type=jnp.float32)
        * gelu_slope
    )
    in_bias_grad = jnp.sum(act_grad, axis=0)
    act_low = act_grad.astype(jnp.bfloat16)
    in_weight_grad = jnp.einsum(
        "rd,rf->df", arrived_flat, act_low, preferred_element_type=jnp.float32
    )
    row_part = jnp.einsum("rf,df->rd", act_low, expert_in[0], preferred_element_type=jnp.float32)
    row_part = row_part.reshape(sources, capacity, feat_dim)
    home_whole = lax.all_to_all(row_part, "dp", split_axis=0, concat_axis=0, tiled=True)
    home_local = jnp.sum(home_whole.reshape(experts, group_size, capacity, feat_dim), axis=1)
    row_back = lax.psum(home_local, "tensor").astype(jnp.bfloat16)
    row_home = (
        row_back.reshape(-1, feat_dim)[slot_index]
        .reshape(tok_count, 2, feat_dim)
        .astype(jnp.float32)
    )
    hidden2_grad = jnp.sum(row_home, axis=1) + jnp.einsum(
        "te,de->td", logit_grad, router, preferred_element_type=jnp.float32
    )
    router_grad = jnp.einsum("td,te->de", hidden2, logit_grad, preferred_element_type=jnp.float32)
    norm2_gain_grad = jnp.sum(hidden2_grad * normed2, axis=0)
    norm2_bias_grad = jnp.sum(hidden2_grad, axis=0)
    middle_grad = grad_out + norm_back(hidden2_grad * norm2_gain, normed2, inverse2)
    proj_bias_grad = jnp.sum(middle_grad, axis=0)
    middle_low = middle_grad.astype(jnp.bfloat16)
    proj_grad = jnp.einsum("tc,td->cd", attended, middle_low, preferred_element_type=jnp.float32)
    attended_grad = jnp.einsum(
        "td,cd->tc", middle_low, proj_weight, preferred_element_type=jnp.float32
    )
    attended_grad = attended_grad.astype(jnp.bfloat16).reshape(images, SEQ, heads_here, HEAD)
    again_scores = (
        jnp.einsum("bqhd,bkhd->bhqk", queries, key_vals, preferred_element_type=jnp.float32)
        * score_scale
    )
    prob_vals = jnp.exp(again_scores - log_total)
    prob_again = prob_vals.astype(jnp.bfloat16)
    value_grad = jnp.einsum(
        "bhqk,bqhd->bkhd", prob_again, attended_grad, preferred_element_type=jnp.float32
    )
    prob_grad = jnp.einsum(
        "bqhd,bkhd->bhqk", attended_grad, values_in, preferred_element_type=jnp.float32
    )
    score_grad = prob_vals * (prob_grad - jnp.sum(prob_vals * prob_grad, axis=-1, keepdims=True))
    score_low = score_grad.astype(jnp.bfloat16)
    query_grad = (
        jnp.einsum("bhqk,bkhd->bqhd", score_low, key_vals, preferred_element_type=jnp.float32)
        * score_scale
    )
    key_grad = (
        jnp.einsum("bhqk,bqhd->bkhd", score_low, queries, preferred_element_type=jnp.float32)
        * score_scale
    )
    proj_low = (
        jnp.stack([query_grad, key_grad, value_grad])
        .reshape(3, tok_count, head_cols)
        .astype(jnp.bfloat16)
    )
    qv_bias_grad = jnp.stack(
        [
            jnp.sum(proj_low[0].astype(jnp.float32), axis=0),
            jnp.sum(proj_low[2].astype(jnp.float32), axis=0),
        ]
    )
    qkv_grad = jnp.einsum("td,jte->jde", hidden1, proj_low, preferred_element_type=jnp.float32)
    hidden1_part = jnp.einsum(
        "jte,jde->td", proj_low, qkv_weight, preferred_element_type=jnp.float32
    )
    hidden1_grad = lax.psum(hidden1_part, "tensor")
    norm1_gain_grad = jnp.sum(hidden1_grad * normed1, axis=0)
    norm1_bias_grad = jnp.sum(hidden1_grad, axis=0)
    input_grad = middle_grad + norm_back(hidden1_grad * norm1_gain, normed1, inverse1)
    summed = lax.psum(
        (
            qkv_grad,
            qv_bias_grad,
            proj_grad,
            proj_bias_grad,
            norm1_gain_grad,
            norm1_bias_grad,
            norm2_gain_grad,
            norm2_bias_grad,
            router_grad,
            out_bias_grad,
        ),
        "dp",
    )
    return (
        output,
        input_grad,
        summed[4],
        summed[5],
        summed[0],
        summed[1],
        summed[2],
        summed[3],
        summed[6],
        summed[7],
        summed[8],
        in_weight_grad[None],
        in_bias_grad[None],
        out_weight_grad[None],
        summed[9],
    )


def solution(mesh):
    return jax.shard_map(
        local,
        mesh=mesh,
        in_specs=(
            P("dp", None),
            P(),
            P(),
            P(None, None, "tensor"),
            P(None, "tensor"),
            P("tensor", None),
            P(),
            P(),
            P(),
            P(),
            P("dp", None, "tensor"),
            P("dp", "tensor"),
            P("dp", "tensor", None),
            P(),
            P("dp", None),
            P("dp", None),
        ),
        out_specs=(
            P("dp", None),
            P("dp", None),
            P(),
            P(),
            P(None, None, "tensor"),
            P(None, "tensor"),
            P("tensor", None),
            P(),
            P(),
            P(),
            P(),
            P("dp", None, "tensor"),
            P("dp", "tensor"),
            P("dp", "tensor", None),
            P(),
        ),
        check_vma=False,
    )
```

profile of v0, /device:TPU:8, one launch (start us, length us, event | category | flops | bytes accessed | tf_op | source)
XLA Modules:
  0.0 654.0 jit_solution(2582611026457275273)
XLA Ops:
  8.1 1.1 convert_reduce_fusion
  9.2 1.2 fusion.31
  11.0 2.3 fusion.13
  15.7 1.2 fusion.63
  17.2 1.2 reduce-window.6
  19.0 29.7 %all-reduce.10.cloned.1.call-done = f32[197,768]{1,0:T(8,128)} async-done(((f32[197,768]{1,0:T(8,128)}), f32[197,768]{1,0:T(8,128)}) %all-reduce.10.cloned.1.call-update) | async-done | bytes 605200 | tf_op jit(solution)/shard_map/psum | solution.py:80
  48.8 1.2 fusion.57
  51.2 1.1 broadcast_in_dim.8
  52.3 2.6 reshape.401
  55.0 3.8 scatter_custom_fusion
  58.7 2.2 reshape_broadcast_in_dim_reshape.6
  60.9 6.1 all-to-all-start
  67.0 2.3 mul.261
  69.3 3.1 mul.262
  72.4 1.1 fusion.64
  74.2 1.4 copy.89
  75.7 1.0 div.60
  76.7 4.0 scatter_custom_fusion.1
  80.8 2.2 reshape_broadcast_in_dim_reshape.7
  83.0 11.1 %all-to-all-done = bf16[16,42,768]{2,1,0:T(8,128)(2,1)} async-done(((bf16[16,42,768]{2,1,0:T(8,128)(2,1)}), bf16[16,42,768]{2,1,0:T(8,128)(2,1)}, u32[]{:S(2)}, u32[]{:S(2)}) %all-to-all-start) | async-done | bytes 1032224 | tf_op jit(solution)/shard_map/all_to_all | solution.py:97
  94.0 5.7 all-to-all-start.2
  99.7 1.3 reduce.13
  101.0 2.2 reshape.373
  103.2 5.1 multiply_convert_fusion
  108.3 18.4 %all-to-all-done.2 = bf16[16,42,768]{2,1,0:T(8,128)(2,1)} async-done(((bf16[16,42,768]{2,1,0:T(8,128)(2,1)}), bf16[16,42,768]{2,1,0:T(8,128)(2,1)}, u32[]{:S(2)}, u32[]{:S(2)}) %all-to-all-start.2) | async-done | bytes 1032224 | tf_op jit(solution)/shard_map/all_to_all | solution.py:129
  126.7 2.2 reshape.375
  129.0 6.7 %fusion.59 = (f32[1536]{0:T(1024)}, bf16[672,1536]{1,0:T(8,128)(2,1)}) fusion(f32[672,1536]{1,0:T(8,128)} %get-tuple-element.111, f32[1536]{0:T(1024)} %reduce.13, bf16[672,768]{1,0:T(8,128)(2,1)} %reshape.375, bf16[1,1536,768]{2,1,0:T(8,128)(2,1)} %param.28), kind=kOutput, calls=%fused_computation.127 | convolution fusion | flops 1597831680 | bytes 9596928 | tf_op jit(solution)/shard_map/rd,fd->rf/dot_general | solution.py:135
  135.7 4.0 dot_general.82
  139.7 5.1 fusion.5
  144.8 5.7 all-to-all-start.3
  150.5 4.0 dot_general.79
  154.6 5.8 fusion.7
  160.3 41.7 %all-to-all-done.3 = f32[16,42,768]{2,1,0:T(8,128)S(1)} async-done(((f32[16,42,768]{2,1,0:T(8,128)}), f32[16,42,768]{2,1,0:T(8,128)S(1)}, u32[]{:S(2)}, u32[]{:S(2)}) %all-to-all-start.3) | async-done | bytes 2064416 | tf_op jit(solution)/shard_map/all_to_all | solution.py:145
  202.0 6.4 all-to-all-start.1
  208.5 1.8 convert_element_type.118
  210.9 49.0 %all-to-all-done.1 = f32[16,42,768]{2,1,0:T(8,128)} async-done(((f32[16,42,768]{2,1,0:T(8,128)}), f32[16,42,768]{2,1,0:T(8,128)}, u32[]{:S(2)}, u32[]{:S(2)}) %all-to-all-start.1) | async-done | bytes 2064416 | tf_op jit(solution)/shard_map/all_to_all | solution.py:107
  260.1 97.1 %all-reduce.19 = bf16[16,42,768]{2,1,0:T(8,128)(2,1)} all-reduce(f32[16,42,768]{2,1,0:T(8,128)S(1)} %all-to-all-done.3), channel_id=1, replica_groups=mesh['dp'=16,'tensor'=2] {'tensor'}, use_global_device_ids=true, to_apply=%region_17.18 | all-reduce | flops 516096 | bytes 3096576 | tf_op jit(solution)/shard_map/psum | solution.py:147
  357.1 1.4 reshape.376
  358.5 2.2 gather_fusion.1
  361.5 2.4 reduce_sum.254
  363.9 2.5 all-reduce.12.cloned.1.call-done
  366.4 1.9 add_convert_fusion
  368.6 2.7 gather_fusion
  371.3 2.0 reshape.379
  373.3 3.5 multiply_reduce_fusion.1
  377.0 2.3 multiply_reduce_fusion.3
  379.3 1.6 fusion.56
  383.8 3.1 convolution_bitcast_fusion.3
  387.0 1.3 fusion.40
  388.4 2.6 convolution_bitcast_fusion.2
  391.3 1.0 copy-done.4
  392.3 0.9 fusion.47
  393.8 6.3 convolution_bitcast_fusion.1
  400.1 4.2 convolution_bitcast_fusion
  406.1 12.9 %all-reduce.14.cloned.1.call-done = f32[197,768]{1,0:T(8,128)} async-done(((f32[197,768]{1,0:T(8,128)}), f32[197,768]{1,0:T(8,128)}) %all-reduce.14.cloned.1.call-update) | async-done | bytes 605200 | tf_op jit(solution)/shard_map/psum | solution.py:204
  419.0 2.1 fusion.30
  421.1 2.1 fusion.29
  423.2 117.6 %all-reduce.18.cloned.1.call-done = (f32[3,768,384]{1,2,0:T(8,128)}, f32[384,768]{1,0:T(8,128)}) async-done(((f32[3,768,384]{1,2,0:T(8,128)}, f32[384,768]{1,0:T(8,128)}), (f32[3,768,384]{1,2,0:T(8,128)}, f32[384,768]{1,0:T(8,128)})) %all-reduce.18.cloned.1.call-update) | async-done | bytes 4718608 | tf_op jit(solution)/shard_map/psum | solution.py:208
  540.8 5.3 copy.104
  546.1 92.2 %all-reduce.16.cloned.1.call-done = (f32[768]{0:T(1024)}, f32[768]{0:T(1024)}, f32[2,384]{1,0:T(2,128)}, f32[768]{0:T(1024)}, f32[768]{0:T(1024)}, /*index=5*/f3...) async-done(((f32[768]{0:T(1024)}, f32[768]{0:T(1024)}, f32[2,384]{1,0:T(2,128)}, f32[768]{0:T(1024)}, f32[768]{0:T(1024)}, /*index=5*/f32[768]{0:T(1024)}, f32[768,16]{0,1:T(8,128)}, ...) | async-done | bytes 116752 | tf_op jit(solution)/shard_map/psum | solution.py:208
  638.3 1.3 copy.128
  639.6 1.3 copy.129
  640.8 1.2 copy.130
  642.1 2.4 copy.131
  (165 shorter events, 17.3 us)
Async XLA Ops:
  7.2 96.0 %copy-start = (bf16[1,768,1536]{2,1,0:T(8,128)(2,1)S(1)}, bf16[1,768,1536]{2,1,0:T(8,128)(2,1)}, u32[]{:S(2)}) copy-start(bf16[1,768,1536]{2,1,0:T(8,128)(2,1)} %param.26) | copy-start | bytes 7077892
  7.2 41.6 %all-reduce.10.cloned.1.call-start = ((), (), s32[]{:S(2)}) async-start(), calls=%async_computation.4 | async-start | bytes 1228800 | tf_op jit(solution)/shard_map/psum | solution.py:80
  10.4 0.6 copy-start.36
  13.5 1.4 copy-start.18
  13.8 0.7 copy-start.14
  14.2 1.0 copy-start.2
  14.5 1.2 copy-start.11
  14.5 2.4 copy-start.28
  15.2 3.8 copy-start.20
  15.2 33.6 %copy-start.5 = (bf16[197,768]{1,0:T(8,128)(2,1)S(1)}, bf16[197,768]{1,0:T(8,128)(2,1)}, u32[]{:S(2)}) copy-start(bf16[197,768]{1,0:T(8,128)(2,1)} %param.16) | copy-start | bytes 907780
  15.2 33.6 %copy-start.39 = (f32[768]{0:T(1024)S(1)}, f32[768]{0:T(1024)}, u32[]{:S(2)}) copy-start(f32[768]{0:T(1024)} %param.22) | copy-start | bytes 9220
  16.9 33.4 %copy-start.26 = (f32[768]{0:T(1024)S(1)}, f32[768]{0:T(1024)}, u32[]{:S(2)}) copy-start(f32[768]{0:T(1024)} %param.23) | copy-start | bytes 9220
  16.9 33.4 %copy-start.40 = (f32[768]{0:T(1024)S(1)}, f32[768]{0:T(1024)}, u32[]{:S(2)}) copy-start(f32[768]{0:T(1024)} %param.24) | copy-start | bytes 9220
  50.3 10.7 %copy-start.32 = (f32[197]{0:T(256)}, f32[197]{0:T(256)S(1)}, u32[]{:S(2)}) copy-start(f32[197]{0:T(256)S(1)} %add_rsqrt_fusion) | copy-start | bytes 2368
  50.5 0.7 copy-start.6
  60.9 33.1 %all-to-all-start = ((bf16[16,42,768]{2,1,0:T(8,128)(2,1)}), bf16[16,42,768]{2,1,0:T(8,128)(2,1)}, u32[]{:S(2)}, u32[]{:S(2)}) async-start(bf16[16,42,768]{2,1,0:T(8,128)(2,1)} %reshape_broadcast_in_dim_reshape.6), calls=%async_computation | async-start | bytes 2359296 | tf_op jit(solution)/shard_map/all_to_all | solution.py:97
  67.0 5.4 copy-start.22
  73.6 0.6 copy-start.34
  76.7 6.2 copy-start.29
  94.0 32.7 %all-to-all-start.2 = ((bf16[16,42,768]{2,1,0:T(8,128)(2,1)}), bf16[16,42,768]{2,1,0:T(8,128)(2,1)}, u32[]{:S(2)}, u32[]{:S(2)}) async-start(bf16[16,42,768]{2,1,0:T(8,128)(2,1)} %reshape_broadcast_in_dim_reshape.7), calls=%async_computation.2 | async-start | bytes 2359296 | tf_op jit(solution)/shard_map/all_to_all | solution.py:129
  144.8 57.2 %all-to-all-start.3 = ((f32[16,42,768]{2,1,0:T(8,128)}), f32[16,42,768]{2,1,0:T(8,128)S(1)}, u32[]{:S(2)}, u32[]{:S(2)}) async-start(f32[16,42,768]{2,1,0:T(8,128)} %fusion.5), calls=%async_computation.3 | async-start | bytes 4718592 | tf_op jit(solution)/shard_map/all_to_all | solution.py:145
  202.0 57.9 %all-to-all-start.1 = ((f32[16,42,768]{2,1,0:T(8,128)}), f32[16,42,768]{2,1,0:T(8,128)}, u32[]{:S(2)}, u32[]{:S(2)}) async-start(f32[16,42,768]{2,1,0:T(8,128)} %fusion.7), calls=%async_computation.1 | async-start | bytes 4718592 | tf_op jit(solution)/shard_map/all_to_all | solution.py:107
  208.5 157.9 %all-reduce.12.cloned.1.call-start = ((), (), s32[]{:S(2)}) async-start(), calls=%async_computation.5 | async-start | bytes 4718592 | tf_op jit(solution)/shard_map/psum | solution.py:109
  260.0 98.5 %copy-start.31 = (s32[1024]{0:T(1024)S(1)}, s32[1024]{0:T(1024)}, u32[]{:S(2)}) copy-start(s32[1024]{0:T(1024)} %pad_clamp_fusion) | copy-start | bytes 12292
  260.0 159.0 %all-reduce.14.cloned.1.call-start = ((), (), s32[]{:S(2)}) async-start(), calls=%async_computation.6 | async-start | bytes 1228800 | tf_op jit(solution)/shard_map/psum | solution.py:204
  360.7 5.7 copy-start.23
  368.6 4.7 copy-start.17
  371.2 2.0 copy-start.9
  371.2 5.6 copy-start.35
  371.3 5.7 copy-start.33
  373.3 6.0 copy-start.8
  376.9 2.4 copy-start.10
  377.0 3.9 copy-start.12
  379.2 2.2 copy-start.3
  380.9 0.9 copy-start.19
  382.2 0.9 copy-start.15
  383.7 3.3 copy-start.21
  386.9 1.4 copy-start.27
  386.9 1.4 copy-start.37
  386.9 1.4 copy-start.44
  387.0 153.8 %all-reduce.18.cloned.1.call-start = ((), (), s32[]{:S(2)}) async-start(), calls=%async_computation.8 | async-start | bytes 9437184 | tf_op jit(solution)/shard_map/psum | solution.py:208
  391.0 1.3 copy-start.4
  391.0 1.3 copy-start.30
  391.0 2.2 copy-start.38
  391.0 247.2 %all-reduce.16.cloned.1.call-start = ((), (), s32[]{:S(2)}) async-start(), calls=%async_computation.7 | async-start | bytes 243712 | tf_op jit(solution)/shard_map/psum | solution.py:208
  393.8 6.3 copy-start.13
  393.8 6.3 copy-start.16
  400.1 5.2 copy-start.7
  540.8 106.7 %copy-start.1 = (bf16[1,768,1536]{2,1,0:T(8,128)(2,1)S(1)}, bf16[1,768,1536]{2,1,0:T(8,128)(2,1)}, u32[]{:S(2)}) copy-start(bf16[1,768,1536]{2,1,0:T(8,128)(2,1)} %param.26) | copy-start | bytes 7077892
  638.3 6.2 copy-start.43
  638.3 6.8 %copy-start.42 = (f32[768]{0:T(1024)S(1)}, f32[768]{0:T(1024)}, u32[]{:S(2)}) copy-start(f32[768]{0:T(1024)} %get-tuple-element.125) | copy-start | bytes 9220
  638.3 7.4 %copy-start.41 = (f32[768]{0:T(1024)S(1)}, f32[768]{0:T(1024)}, u32[]{:S(2)}) copy-start(f32[768]{0:T(1024)} %get-tuple-element.126) | copy-start | bytes 9220
  638.3 8.0 %copy-start.25 = (f32[768,16]{0,1:T(8,128)S(1)}, f32[768,16]{0,1:T(8,128)}, u32[]{:S(2)}) copy-start(f32[768,16]{0,1:T(8,128)} %get-tuple-element.127) | copy-start | bytes 147460
  638.3 8.6 %copy-start.24 = (f32[16,768]{1,0:T(8,128)S(1)}, f32[16,768]{1,0:T(8,128)}, u32[]{:S(2)}) copy-start(f32[16,768]{1,0:T(8,128)} %get-tuple-element.131) | copy-start | bytes 147460
Sparse Core Ops, SparseCore 0:
  17.0 31.7 all-reduce.9
  260.1 106.2 all-reduce.11
  387.1 31.8 all-reduce.13
  423.5 117.2 all-reduce.17
  546.8 91.3 all-reduce.15
where the time goes:
time: 656 us; the launch traced here: 654 us
  waiting for transfers between devices  375 us (57%)
  blocking collectives  97.1 us (15%)
  local copies, waits for them, and re-layouts  63 us (10%)
  matrix products  51.2 us (8%)
  other arithmetic  28.9 us (4%)
  starting transfers between devices  24.3 us (4%)
  between operations  14.3 us (2%)
    psum x2, waiting for transfers between devices, local(): lax.psum((qkv_grad, qv_bias_grad, proj_grad, proj_bias_grad, norm1_gain_g...  210 us
    psum x1, blocking collectives, local(): row_back = lax.psum(home_local, 'tensor').astype(jnp.bfloat16)  97.1 us
    all_to_all x1, waiting for transfers between devices, local(): lax.all_to_all(part_out, 'dp', split_axis=0, concat_axis=0, tiled=True)  49 us
    all_to_all x1, waiting for transfers between devices, local(): lax.all_to_all(row_part, 'dp', split_axis=0, concat_axis=0, tiled=True)  41.7 us
    psum x1, waiting for transfers between devices, local(): middle = x_in + lax.psum(attn_part, 'tensor') + proj_bias  29.7 us
    all_to_all x1, waiting for transfers between devices, local(): lax.all_to_all(send_grad_all, 'dp', split_axis=0, concat_axis=0, tiled=True)  18.4 us
    unnamed x101, local copies, waits for them, and re-layouts  18.2 us
  transfers between devices with their start and end apart: 9, of which 9 were waited for; matrix products, arithmetic and copies ran while one was open for 11% of the time, Pallas kernels for 0%

commit v1 on v0

--- a/solution.py
+++ b/solution.py
@@ -144,7 +144,7 @@
     row_part = row_part.reshape(sources, capacity, feat_dim)
     home_whole = lax.all_to_all(row_part, "dp", split_axis=0, concat_axis=0, tiled=True)
     home_local = jnp.sum(home_whole.reshape(experts, group_size, capacity, feat_dim), axis=1)
-    row_back = lax.psum(home_local, "tensor").astype(jnp.bfloat16)
+    row_back = jnp.sum(lax.all_gather(home_local, "tensor"), axis=0).astype(jnp.bfloat16)
     row_home = (
         row_back.reshape(-1, feat_dim)[slot_index]
         .reshape(tok_count, 2, feat_dim)

time: 656 us -> 614 us (0.936); the launches traced: 654 us -> 604 us
  blocking collectives: 97.1 us -> 0 us
  waiting for transfers between devices: 375 us -> 419 us
    psum x1 -> x0, blocking collectives: 97.1 us -> none  [local(): row_back = lax.psum(home_local, 'tensor').astype(jnp.bfloat16)]
    all_gather x0 -> x1, waiting for transfers between devices: none -> 47.7 us  [local(): lax.all_gather(home_local, 'tensor')]
    all_to_all x1, waiting for transfers between devices: 49 us -> 33.5 us  [local(): lax.all_to_all(part_out, 'dp', split_axis=0, concat_axis=0, tiled=True)]
    psum x1, waiting for transfers between devices: 2.51 us -> 16.1 us  [local(): full_rows = lax.psum(local_rows, 'tensor') + expert_out_bias[:, None, :]]
    all_to_all x1, waiting for transfers between devices: 18.4 us -> 8.41 us  [local(): lax.all_to_all(send_grad_all, 'dp', split_axis=0, concat_axis=0, tiled=True)]
    all_to_all x1, waiting for transfers between devices: 41.7 us -> 50.7 us  [local(): lax.all_to_all(row_part, 'dp', split_axis=0, concat_axis=0, tiled=True)]
    unnamed x101 -> x97, local copies, waits for them, and re-layouts: 18.2 us -> 19 us
  transfers between devices with their start and end apart: 9 -> 10, of which waited for: 9 -> 10; matrix products, arithmetic and copies ran while one was open for 11% -> 16% of each run, Pallas kernels for 0% -> 0%
where the time goes in v1:
time: 614 us; the launch traced here: 604 us
  waiting for transfers between devices  419 us (68%)
  local copies, waits for them, and re-layouts  65.6 us (11%)
  matrix products  50 us (8%)
  other arithmetic  29 us (5%)
  starting transfers between devices  25.2 us (4%)
  between operations  14.9 us (2%)
    psum x2, waiting for transfers between devices, local(): lax.psum((qkv_grad, qv_bias_grad, proj_grad, proj_bias_grad, norm1_gain_g...  210 us
    all_to_all x1, waiting for transfers between devices, local(): lax.all_to_all(row_part, 'dp', split_axis=0, concat_axis=0, tiled=True)  50.7 us
    all_gather x1, waiting for transfers between devices, local(): lax.all_gather(home_local, 'tensor')  47.7 us
    all_to_all x1, waiting for transfers between devices, local(): lax.all_to_all(part_out, 'dp', split_axis=0, concat_axis=0, tiled=True)  33.5 us
    psum x1, waiting for transfers between devices, local(): middle = x_in + lax.psum(attn_part, 'tensor') + proj_bias  29.7 us
    unnamed x97, local copies, waits for them, and re-layouts  19 us
    psum x1, waiting for transfers between devices, local(): full_rows = lax.psum(local_rows, 'tensor') + expert_out_bias[:, None, :]  16.1 us
  transfers between devices with their start and end apart: 10, of which 10 were waited for; matrix products, arithmetic and copies ran while one was open for 16% of the time, Pallas kernels for 0%

profile of v1, /device:TPU:8, one launch (start us, length us, event | category | flops | bytes accessed | tf_op | source)
XLA Modules:
  0.0 603.9 jit_solution(4496185938288408508)
XLA Ops:
  8.1 1.1 convert_reduce_fusion
  9.2 1.2 fusion.31
  11.0 2.3 fusion.13
  15.7 1.2 fusion.63
  17.2 1.2 reduce-window.6
  19.0 29.7 %all-reduce.9.cloned.1.call-done = f32[197,768]{1,0:T(8,128)} async-done(((f32[197,768]{1,0:T(8,128)}), f32[197,768]{1,0:T(8,128)}) %all-reduce.9.cloned.1.call-update) | async-done | bytes 605200 | tf_op jit(solution)/shard_map/psum | solution.py:80
  48.8 1.2 fusion.57
  51.2 1.1 broadcast_in_dim.8
  52.3 2.6 reshape.401
  55.0 3.8 scatter_custom_fusion
  58.7 2.2 reshape_broadcast_in_dim_reshape.6
  60.9 6.1 %all-to-all-start = ((bf16[16,42,768]{2,1,0:T(8,128)(2,1)}), bf16[16,42,768]{2,1,0:T(8,128)(2,1)}, u32[]{:S(2)}, u32[]{:S(2)}) async-start(bf16[16,42,768]{2,1,0:T(8,128)(2,1)} %reshape_broadcast_in_dim_reshape.6), calls=%async_computation | async-start | bytes 2359296 | tf_op jit(solution)/shard_map/all_to_all | solution.py:97
  67.0 2.3 mul.261
  69.3 3.1 mul.262
  72.4 1.1 fusion.64
  74.2 1.4 copy.130
  75.7 1.0 div.60
  76.7 4.0 scatter_custom_fusion.1
  80.7 2.2 reshape_broadcast_in_dim_reshape.7
  83.0 11.0 %all-to-all-done = bf16[16,42,768]{2,1,0:T(8,128)(2,1)} async-done(((bf16[16,42,768]{2,1,0:T(8,128)(2,1)}), bf16[16,42,768]{2,1,0:T(8,128)(2,1)}, u32[]{:S(2)}, u32[]{:S(2)}) %all-to-all-start) | async-done | bytes 1032224 | tf_op jit(solution)/shard_map/all_to_all | solution.py:97
  94.0 6.3 %all-to-all-start.2 = ((bf16[16,42,768]{2,1,0:T(8,128)(2,1)}), bf16[16,42,768]{2,1,0:T(8,128)(2,1)}, u32[]{:S(2)}, u32[]{:S(2)}) async-start(bf16[16,42,768]{2,1,0:T(8,128)(2,1)} %reshape_broadcast_in_dim_reshape.7), calls=%async_computation.2 | async-start | bytes 2359296 | tf_op jit(solution)/shard_map/all_to_all | solution.py:129
  100.3 1.3 reduce.13
  101.6 2.2 reshape.374
  103.9 5.1 multiply_convert_fusion
  109.0 4.0 dot_general.79
  113.0 5.8 fusion.7
  118.8 8.4 %all-to-all-done.2 = bf16[16,42,768]{2,1,0:T(8,128)(2,1)} async-done(((bf16[16,42,768]{2,1,0:T(8,128)(2,1)}), bf16[16,42,768]{2,1,0:T(8,128)(2,1)}, u32[]{:S(2)}, u32[]{:S(2)}) %all-to-all-start.2) | async-done | bytes 1032224 | tf_op jit(solution)/shard_map/all_to_all | solution.py:129
  127.2 5.7 all-to-all-start.1
  132.9 2.2 reshape.376
  135.1 6.7 %fusion.59 = (f32[1536]{0:T(1024)}, bf16[672,1536]{1,0:T(8,128)(2,1)}) fusion(f32[672,1536]{1,0:T(8,128)} %get-tuple-element.141, f32[1536]{0:T(1024)} %reduce.13, bf16[672,768]{1,0:T(8,128)(2,1)} %reshape.376, bf16[1,1536,768]{2,1,0:T(8,128)(2,1)} %param.28), kind=kOutput, calls=%fused_computation.127 | convolution fusion | flops 1597831680 | bytes 9596928 | tf_op jit(solution)/shard_map/rd,fd->rf/dot_general | solution.py:135
  141.8 4.0 dot_general.82
  145.8 5.1 fusion.5
  150.9 33.5 %all-to-all-done.1 = f32[16,42,768]{2,1,0:T(8,128)} async-done(((f32[16,42,768]{2,1,0:T(8,128)}), f32[16,42,768]{2,1,0:T(8,128)}, u32[]{:S(2)}, u32[]{:S(2)}) %all-to-all-start.1) | async-done | bytes 2064416 | tf_op jit(solution)/shard_map/all_to_all | solution.py:107
  184.4 6.6 %all-to-all-start.3 = ((f32[16,42,768]{2,1,0:T(8,128)}), f32[16,42,768]{2,1,0:T(8,128)S(1)}, u32[]{:S(2)}, u32[]{:S(2)}) async-start(f32[16,42,768]{2,1,0:T(8,128)} %fusion.5), calls=%async_computation.3 | async-start | bytes 4718592 | tf_op jit(solution)/shard_map/all_to_all | solution.py:145
  191.7 50.7 %all-to-all-done.3 = f32[16,42,768]{2,1,0:T(8,128)S(1)} async-done(((f32[16,42,768]{2,1,0:T(8,128)}), f32[16,42,768]{2,1,0:T(8,128)S(1)}, u32[]{:S(2)}, u32[]{:S(2)}) %all-to-all-start.3) | async-done | bytes 2064416 | tf_op jit(solution)/shard_map/all_to_all | solution.py:145
  242.4 2.5 copy.136
  246.8 16.1 %all-reduce.11.cloned.1.call-done = f32[16,42,768]{2,1,0:T(8,128)} async-done(((f32[16,42,768]{2,1,0:T(8,128)}), f32[16,42,768]{2,1,0:T(8,128)}) %all-reduce.11.cloned.1.call-update) | async-done | bytes 2064400 | tf_op jit(solution)/shard_map/psum | solution.py:109
  262.9 1.9 add_convert_fusion
  265.1 2.7 gather_fusion
  267.7 2.0 reshape.379
  269.7 3.5 multiply_reduce_fusion.1
  273.4 47.7 %all-gather.3.cloned.1.call-done = f32[32,42,768]{2,0,1:T(8,128)} async-done(((f32[16,42,768]{2,0,1:T(8,128)}), f32[32,42,768]{2,0,1:T(8,128)}) %all-gather.3.cloned.1.call-update) | async-done | bytes 4128784 | tf_op jit(solution)/shard_map/all_gather | solution.py:147
  321.1 2.6 reduce_sum.263
  324.4 2.2 gather_fusion.1
  327.4 1.4 reduce_sum.264
  328.8 1.0 multiply_reduce_fusion.3
  329.9 1.6 fusion.56
  334.5 3.1 convolution_bitcast_fusion.3
  337.6 1.3 fusion.40
  339.0 2.6 convolution_bitcast_fusion.2
  341.9 1.0 copy-done.4
  342.9 0.9 fusion.47
  344.4 6.3 %convolution_bitcast_fusion.1 = f32[1,768,1536]{2,1,0:T(8,128)} fusion(bf16[672,768]{1,0:T(8,128)(2,1)} %reshape.374, bf16[672,1536]{1,0:T(8,128)(2,1)} %get-tuple-element.130), kind=kOutput, calls=%fused_computation.13 | convolution fusion | flops 1585446912 | bytes 7815168 | tf_op jit(solution)/shard_map/rd,rf->df/dot_general | solution.py:140
  350.7 4.2 convolution_bitcast_fusion
  356.7 11.6 %all-reduce.13.cloned.1.call-done = f32[197,768]{1,0:T(8,128)} async-done(((f32[197,768]{1,0:T(8,128)}), f32[197,768]{1,0:T(8,128)}) %all-reduce.13.cloned.1.call-update) | async-done | bytes 605200 | tf_op jit(solution)/shard_map/psum | solution.py:204
  368.3 2.1 fusion.30
  370.4 2.1 fusion.29
  372.6 117.6 %all-reduce.17.cloned.1.call-done = (f32[3,768,384]{1,2,0:T(8,128)}, f32[384,768]{1,0:T(8,128)}) async-done(((f32[3,768,384]{1,2,0:T(8,128)}, f32[384,768]{1,0:T(8,128)}), (f32[3,768,384]{1,2,0:T(8,128)}, f32[384,768]{1,0:T(8,128)})) %all-reduce.17.cloned.1.call-update) | async-done | bytes 4718608 | tf_op jit(solution)/shard_map/psum | solution.py:208
  490.2 5.3 copy.147
  495.5 92.1 %all-reduce.15.cloned.1.call-done = (f32[768]{0:T(1024)}, f32[768]{0:T(1024)}, f32[2,384]{1,0:T(2,128)}, f32[768]{0:T(1024)}, f32[768]{0:T(1024)}, /*index=5*/f3...) async-done(((f32[768]{0:T(1024)}, f32[768]{0:T(1024)}, f32[2,384]{1,0:T(2,128)}, f32[768]{0:T(1024)}, f32[768]{0:T(1024)}, /*index=5*/f32[768]{0:T(1024)}, f32[768,16]{0,1:T(8,128)}, ...) | async-done | bytes 116752 | tf_op jit(solution)/shard_map/psum | solution.py:208
  587.6 1.3 copy.169
  588.9 1.3 copy.170
  590.2 1.2 copy.171
  591.4 2.4 copy.172
  (166 shorter events, 19.9 us)
Async XLA Ops:
  7.2 96.7 %copy-start = (bf16[1,768,1536]{2,1,0:T(8,128)(2,1)S(1)}, bf16[1,768,1536]{2,1,0:T(8,128)(2,1)}, u32[]{:S(2)}) copy-start(bf16[1,768,1536]{2,1,0:T(8,128)(2,1)} %param.26) | copy-start | bytes 7077892
  7.2 41.6 %all-reduce.9.cloned.1.call-start = ((), (), s32[]{:S(2)}) async-start(), calls=%async_computation.4 | async-start | bytes 1228800 | tf_op jit(solution)/shard_map/psum | solution.py:80
  10.4 0.6 copy-start.32
  13.5 1.4 copy-start.19
  13.8 0.7 copy-start.15
  14.2 1.0 copy-start.2
  14.5 1.2 copy-start.12
  14.5 2.4 copy-start.29
  15.2 3.8 copy-start.21
  15.2 33.5 %copy-start.5 = (bf16[197,768]{1,0:T(8,128)(2,1)S(1)}, bf16[197,768]{1,0:T(8,128)(2,1)}, u32[]{:S(2)}) copy-start(bf16[197,768]{1,0:T(8,128)(2,1)} %param.16) | copy-start | bytes 907780
  15.2 33.5 %copy-start.37 = (f32[768]{0:T(1024)S(1)}, f32[768]{0:T(1024)}, u32[]{:S(2)}) copy-start(f32[768]{0:T(1024)} %param.22) | copy-start | bytes 9220
  16.9 33.4 %copy-start.27 = (f32[768]{0:T(1024)S(1)}, f32[768]{0:T(1024)}, u32[]{:S(2)}) copy-start(f32[768]{0:T(1024)} %param.23) | copy-start | bytes 9220
  16.9 33.4 %copy-start.38 = (f32[768]{0:T(1024)S(1)}, f32[768]{0:T(1024)}, u32[]{:S(2)}) copy-start(f32[768]{0:T(1024)} %param.24) | copy-start | bytes 9220
  19.0 35.9 %copy-start.34 = (s32[394,1]{0,1:T(1,128)}, s32[394,1]{0,1:T(1,128)S(1)}, u32[]{:S(2)}) copy-start(s32[394,1]{0,1:T(1,128)S(1)} %compare_select_fusion) | copy-start | bytes 4732
  50.4 0.7 copy-start.6
  60.9 33.1 %all-to-all-start = ((bf16[16,42,768]{2,1,0:T(8,128)(2,1)}), bf16[16,42,768]{2,1,0:T(8,128)(2,1)}, u32[]{:S(2)}, u32[]{:S(2)}) async-start(bf16[16,42,768]{2,1,0:T(8,128)(2,1)} %reshape_broadcast_in_dim_reshape.6), calls=%async_computation | async-start | bytes 2359296 | tf_op jit(solution)/shard_map/all_to_all | solution.py:97
  67.0 5.4 copy-start.23
  73.6 0.6 copy-start.30
  94.0 33.2 %all-to-all-start.2 = ((bf16[16,42,768]{2,1,0:T(8,128)(2,1)}), bf16[16,42,768]{2,1,0:T(8,128)(2,1)}, u32[]{:S(2)}, u32[]{:S(2)}) async-start(bf16[16,42,768]{2,1,0:T(8,128)(2,1)} %reshape_broadcast_in_dim_reshape.7), calls=%async_computation.2 | async-start | bytes 2359296 | tf_op jit(solution)/shard_map/all_to_all | solution.py:129
  127.2 57.2 %all-to-all-start.1 = ((f32[16,42,768]{2,1,0:T(8,128)}), f32[16,42,768]{2,1,0:T(8,128)}, u32[]{:S(2)}, u32[]{:S(2)}) async-start(f32[16,42,768]{2,1,0:T(8,128)} %fusion.7), calls=%async_computation.1 | async-start | bytes 4718592 | tf_op jit(solution)/shard_map/all_to_all | solution.py:107
  184.4 58.1 %all-to-all-start.3 = ((f32[16,42,768]{2,1,0:T(8,128)}), f32[16,42,768]{2,1,0:T(8,128)S(1)}, u32[]{:S(2)}, u32[]{:S(2)}) async-start(f32[16,42,768]{2,1,0:T(8,128)} %fusion.5), calls=%async_computation.3 | async-start | bytes 4718592 | tf_op jit(solution)/shard_map/all_to_all | solution.py:145
  190.9 71.9 %all-reduce.11.cloned.1.call-start = ((), (), s32[]{:S(2)}) async-start(), calls=%async_computation.5 | async-start | bytes 4718592 | tf_op jit(solution)/shard_map/psum | solution.py:109
  191.7 129.4 %all-gather.3.cloned.1.call-start = ((), (), s32[]{:S(2)}) async-start(), calls=%async_computation.7 | async-start | bytes 6193152 | tf_op jit(solution)/shard_map/all_gather | solution.py:147
  244.9 1.0 copy-start.8
  244.9 1.8 copy-start.35
  244.9 17.9 %copy-start.24 = (f32[16,768]{1,0:T(8,128)S(1)}, f32[16,768]{1,0:T(8,128)}, u32[]{:S(2)}) copy-start(f32[16,768]{1,0:T(8,128)} %param.29) | copy-start | bytes 147460
  245.0 123.3 %all-reduce.13.cloned.1.call-start = ((), (), s32[]{:S(2)}) async-start(), calls=%async_computation.6 | async-start | bytes 1228800 | tf_op jit(solution)/shard_map/psum | solution.py:204
  265.1 4.7 copy-start.18
  267.7 2.0 copy-start.10
  267.7 5.6 copy-start.31
  327.4 2.5 copy-start.9
  328.8 1.1 copy-start.11
  328.8 2.7 copy-start.13
  329.9 2.1 copy-start.3
  331.5 0.9 copy-start.20
  332.8 0.9 copy-start.16
  334.3 3.3 copy-start.22
  337.6 1.4 copy-start.28
  337.6 1.4 copy-start.33
  337.6 1.4 copy-start.42
  337.6 152.6 %all-reduce.17.cloned.1.call-start = ((), (), s32[]{:S(2)}) async-start(), calls=%async_computation.9 | async-start | bytes 9437184 | tf_op jit(solution)/shard_map/psum | solution.py:208
  341.6 1.3 copy-start.4
  341.6 2.2 copy-start.36
  341.7 245.9 %all-reduce.15.cloned.1.call-start = ((), (), s32[]{:S(2)}) async-start(), calls=%async_computation.8 | async-start | bytes 243712 | tf_op jit(solution)/shard_map/psum | solution.py:208
  344.4 6.3 %copy-start.14 = (bf16[672,1536]{1,0:T(8,128)(2,1)S(1)}, bf16[672,1536]{1,0:T(8,128)(2,1)}, u32[]{:S(2)}) copy-start(bf16[672,1536]{1,0:T(8,128)(2,1)} %get-tuple-element.140) | copy-start | bytes 6193156
  344.4 6.3 %copy-start.17 = (bf16[672,768]{1,0:T(8,128)(2,1)S(1)}, bf16[672,768]{1,0:T(8,128)(2,1)}, u32[]{:S(2)}) copy-start(bf16[672,768]{1,0:T(8,128)(2,1)} %reshape.376) | copy-start | bytes 3096580
  350.7 4.2 copy-start.7
  490.2 106.7 %copy-start.1 = (bf16[1,768,1536]{2,1,0:T(8,128)(2,1)S(1)}, bf16[1,768,1536]{2,1,0:T(8,128)(2,1)}, u32[]{:S(2)}) copy-start(bf16[1,768,1536]{2,1,0:T(8,128)(2,1)} %param.26) | copy-start | bytes 7077892
  587.6 6.2 %copy-start.41 = (f32[768]{0:T(1024)S(1)}, f32[768]{0:T(1024)}, u32[]{:S(2)}) copy-start(f32[768]{0:T(1024)} %get-tuple-element.154) | copy-start | bytes 9220
  587.6 6.8 %copy-start.40 = (f32[768]{0:T(1024)S(1)}, f32[768]{0:T(1024)}, u32[]{:S(2)}) copy-start(f32[768]{0:T(1024)} %get-tuple-element.155) | copy-start | bytes 9220
  587.6 7.4 %copy-start.39 = (f32[768]{0:T(1024)S(1)}, f32[768]{0:T(1024)}, u32[]{:S(2)}) copy-start(f32[768]{0:T(1024)} %get-tuple-element.156) | copy-start | bytes 9220
  587.6 8.0 %copy-start.26 = (f32[768,16]{0,1:T(8,128)S(1)}, f32[768,16]{0,1:T(8,128)}, u32[]{:S(2)}) copy-start(f32[768,16]{0,1:T(8,128)} %get-tuple-element.157) | copy-start | bytes 147460
  587.6 8.6 %copy-start.25 = (f32[16,768]{1,0:T(8,128)S(1)}, f32[16,768]{1,0:T(8,128)}, u32[]{:S(2)}) copy-start(f32[16,768]{1,0:T(8,128)} %get-tuple-element.161) | copy-start | bytes 147460
Sparse Core Ops, SparseCore 0:
  17.0 31.7 all-reduce.8
  194.1 68.7 all-reduce.10
  265.1 56.0 all-gather.2
  337.7 30.5 all-reduce.12
  372.9 117.2 all-reduce.16
  496.2 91.3 all-reduce.14
